TPU v7x, 256 devices: a whole 4x4x8 slice. The times are simulated.
256 devices in a mesh: row: 8 (over y, core), col: 32 (over x, z).
Axes of the slice: x: 4, y: 4, z: 8, core: 2. Of those that a mesh axis runs over, the one named last changes fastest.
Arguments:
- columns: float32 [2048, 131072], P(None, ('row', 'col')), may hold values from -6000 to 6000
- seating: int32 [32], replicated, may hold values from 0 to 31, each once
Outputs:
- rotated: float32 [2048, 131072], P(None, ('row', 'col'))
All inputs are finite; a program needn't handle non-finite values.
Results may differ from a plain program's by a relative error of at most 0.0001.
Values sent between devices are 32-bit elements; how exact they have to be, the bound alone decides.
No kernel may reach another device: no remote copies, remote signals or barrier semaphores. Data moves between devices by JAX's collectives and lax.ppermute only.
A program may use at most 128 MiB of HBM per device.

v0:
```python
import jax
import jax.numpy as jnp
from jax import lax
from jax.sharding import PartitionSpec as P

BLOCK = 64
NS_STEPS = 5
highest = lax.Precision.HIGHEST


def rotation(pair_gram, total_rows):
    pair_width = pair_gram.shape[-1]
    frobenius = jnp.sqrt(jnp.sum(pair_gram * pair_gram, axis=(-2, -1), keepdims=True))
    current = pair_gram / frobenius
    identity = jnp.eye(pair_width, dtype=jnp.float32)
    inverse_root = jnp.broadcast_to(identity, pair_gram.shape)
    for newton_turn in range(NS_STEPS):
        factor = 1.5 * identity - 0.5 * jnp.matmul(inverse_root, current, precision=highest)
        current = jnp.matmul(current, factor, precision=highest)
        inverse_root = jnp.matmul(factor, inverse_root, precision=highest)
    return inverse_root * jnp.sqrt(total_rows / frobenius)


def pair_up(blocks, stride):
    count = blocks.shape[0]
    shaped = blocks.reshape(count // (2 * stride), 2, stride, blocks.shape[1], blocks.shape[2])
    return jnp.concatenate([shaped[:, 0], shaped[:, 1]], axis=2)


def split_pairs(rotated_pairs, stride):
    groups = rotated_pairs.shape[0]
    half_width = rotated_pairs.shape[2] // 2
    shaped = rotated_pairs.reshape(groups, stride, 2, half_width, rotated_pairs.shape[3])
    return jnp.transpose(shaped, (0, 2, 1, 3, 4)).reshape(
        groups * 2 * stride, half_width, rotated_pairs.shape[3]
    )


def body(columns, seating):
    block_count = seating.shape[0]
    rows_here = columns.shape[1]
    col_count = lax.axis_size("col")
    total_rows = float(rows_here * lax.axis_size("row") * col_count)
    seat_count = block_count // col_count
    seated = columns.reshape(block_count, BLOCK, rows_here)[seating].reshape(
        block_count * BLOCK, rows_here
    )
    current = seated.reshape(block_count, BLOCK, rows_here)
    for stride in (seat_count, block_count // 2):
        paired = pair_up(current, stride)
        partial_gram = jnp.einsum("gsam,gsbm->gsab", paired, paired, precision=highest)
        pair_gram = lax.psum(partial_gram, ("row", "col"))
        rotate = rotation(pair_gram, total_rows)
        moved = jnp.einsum("gsab,gsam->gsbm", rotate, paired, precision=highest)
        current = split_pairs(moved, stride)
    seated = current.reshape(block_count * BLOCK, rows_here)
    ordered = seated.reshape(block_count, BLOCK, rows_here)
    restored = jnp.zeros_like(ordered).at[seating].set(ordered)
    return restored.reshape(block_count * BLOCK, rows_here)


def solution(mesh):
    in_specs = (P(None, ("row", "col")), P())
    out_specs = P(None, ("row", "col"))
    return jax.shard_map(body, mesh=mesh, in_specs=in_specs, out_specs=out_specs, check_vma=False)
```

profile of v0, /device:TPU:2, one launch (start us, length us, event | category | flops | bytes accessed | tf_op | source)
XLA Modules:
  0.0 617.4 jit_solution(11122427788383581620)
XLA Ops:
  6.5 0.7 compare_select_fusion
  7.2 5.0 gather_fusion
  12.2 2.7 slice_bitcast_fusion.3
  15.0 1.3 copy-done
  16.3 5.0 fusion.4
  21.3 0.0 all-reduce.3.cloned.1.call-update
  21.3 0.2 all-reduce.5.cloned.1.call-start
  21.6 261.7 %all-reduce.3.cloned.1.call-done = f32[16,1,128,128]{3,2,0,1:T(8,128)} async-done(((f32[16,1,128,128]{3,2,0,1:T(8,128)}), f32[16,1,128,128]{3,2,0,1:T(8,128)}) %all-reduce.3.cloned.1.call-update) | async-done | bytes 1048592 | tf_op jit(solution)/shard_map/psum | solution.py:52
  283.3 1.5 multiply_reduce_fusion.1
  284.9 2.3 fusion.15
  287.2 1.0 fusion.25
  288.2 1.3 fusion.19
  289.5 1.2 fusion.14
  290.7 1.2 fusion.35
  291.9 1.2 fusion.34
  293.1 1.2 fusion.13
  294.3 1.2 fusion.37
  295.5 1.2 fusion.36
  296.7 1.4 fusion.12
  298.2 1.2 fusion.38
  299.4 1.2 fusion.39
  300.6 1.2 fusion.11
  301.8 1.9 convolution_multiply_fusion.6
  303.7 3.8 fusion.2
  307.5 0.5 slice_bitcast_fusion.1
  308.0 1.3 copy-done.2
  309.3 5.5 fusion.5
  314.8 0.0 all-reduce.5.cloned.1.call-update
  314.8 257.9 %all-reduce.5.cloned.1.call-done = f32[1,16,128,128]{3,2,1,0:T(8,128)} async-done(((f32[1,16,128,128]{3,2,1,0:T(8,128)}), f32[1,16,128,128]{3,2,1,0:T(8,128)}) %all-reduce.5.cloned.1.call-update) | async-done | bytes 1048592 | tf_op jit(solution)/shard_map/psum | solution.py:52
  572.8 1.5 multiply_reduce_fusion
  574.3 2.3 fusion.10
  576.7 1.0 fusion.22
  577.7 1.3 fusion.16
  579.0 1.2 fusion.9
  580.2 1.2 fusion.41
  581.4 1.2 fusion.40
  582.6 1.2 fusion.8
  583.8 1.2 fusion.43
  585.0 1.4 fusion.42
  586.3 1.2 fusion.7
  587.6 1.2 fusion.44
  588.8 1.2 fusion.45
  590.0 1.2 fusion.6
  591.2 1.9 convolution_multiply_fusion
  593.1 3.8 fusion
  596.9 2.6 copy.5
  599.5 2.5 broadcast_in_dim.4
  602.1 8.3 %scatter_fusion = f32[32,64,512]{2,1,0:T(8,128)} fusion(f32[32,64,512]{2,1,0:T(8,128)} %broadcast_in_dim.4, s32[32]{0:T(128)S(1)} %compare_select_fusion, f32[32,64,512]{2,1,0:T(8,128)} %bitcast.98), kind=kCustom, calls=%fused_computation.1 | custom fusion | bytes 12583040 | tf_op jit(solution)/shard_map/scatter | solution.py:58
  (16 shorter events, 0.1 us)
Async XLA Ops:
  6.5 276.8 %all-reduce.3.cloned.1.call-start = ((), (), s32[]{:S(2)}) async-start(), calls=%async_computation | async-start | bytes 2097152 | tf_op jit(solution)/shard_map/psum | solution.py:52
  15.0 1.3 copy-start
  21.3 551.4 %all-reduce.5.cloned.1.call-start = ((), (), s32[]{:S(2)}) async-start(), calls=%async_computation.1 | async-start | bytes 2097152 | tf_op jit(solution)/shard_map/psum | solution.py:52
  283.3 4.9 copy-start.4
  299.4 4.3 copy-start.1
  308.0 1.3 copy-start.2
  572.8 4.9 copy-start.5
  588.8 4.3 copy-start.3
Sparse Core Ops, SparseCore 0:
  21.4 261.8 all-reduce.2
  315.0 257.7 all-reduce.4
where the time goes:
time: 622 us; the launch traced here: 617 us
  waiting for transfers between devices  520 us (84%)
  matrix products  55.4 us (9%)
  local copies, waits for them, and re-layouts  24.4 us (4%)
  between operations  13.9 us (2%)
    psum x2, waiting for transfers between devices, body(): pair_gram = lax.psum(partial_gram, ('row', 'col'))  520 us
    dot_general x10, matrix products, rotation(): jnp.matmul(inverse_root, current, precision=highest)  14.6 us
    dot_general x10, matrix products, rotation(): inverse_root = jnp.matmul(factor, inverse_root, precision=highest)  13.1 us
  transfers between devices with their start and end apart: 2, of which 2 were waited for; matrix products, arithmetic and copies ran while one was open for 0% of the time, Pallas kernels for 0%

commit v1 on v0

--- a/solution.py
+++ b/solution.py
@@ -49,7 +49,7 @@
     for stride in (seat_count, block_count // 2):
         paired = pair_up(current, stride)
         partial_gram = jnp.einsum("gsam,gsbm->gsab", paired, paired, precision=highest)
-        pair_gram = lax.psum(partial_gram, ("row", "col"))
+        pair_gram = lax.psum(lax.psum(partial_gram, "row"), "col")
         rotate = rotation(pair_gram, total_rows)
         moved = jnp.einsum("gsab,gsam->gsbm", rotate, paired, precision=highest)
         current = split_pairs(moved, stride)

time: 622 us -> 544 us (0.87)
  waiting for transfers between devices: 520 us -> 441 us
    psum x2 -> x4, waiting for transfers between devices: 520 us -> 441 us  [body(): pair_gram = lax.psum(lax.psum(partial_gram, 'row'), 'col')]
  transfers between devices with their start and end apart: 2 -> 4, of which waited for: 2 -> 4; matrix products, arithmetic and copies ran while one was open for 0% -> 0% of each run, Pallas kernels for 0% -> 0%
where the time goes in v1:
time: 544 us; the launch traced here: 538 us
  waiting for transfers between devices  441 us (81%)
  matrix products  55.3 us (10%)
  local copies, waits for them, and re-layouts  24.4 us (4%)
  between operations  13.7 us (3%)
    psum x4, waiting for transfers between devices, body(): pair_gram = lax.psum(lax.psum(partial_gram, 'row'), 'col')  441 us
    dot_general x10, matrix products, rotation(): jnp.matmul(inverse_root, current, precision=highest)  15 us
    dot_general x10, matrix products, rotation(): inverse_root = jnp.matmul(factor, inverse_root, precision=highest)  13 us
  transfers between devices with their start and end apart: 4, of which 4 were waited for; matrix products, arithmetic and copies ran while one was open for 0% of the time, Pallas kernels for 0%

profile of v1, /device:TPU:2, one launch (start us, length us, event | category | flops | bytes accessed | tf_op | source)
XLA Modules:
  0.0 538.1 jit_solution(4107555459800619245)
XLA Ops:
  6.5 0.7 compare_select_fusion
  7.2 5.0 gather_fusion
  12.2 2.7 slice_bitcast_fusion.3
  15.0 1.3 copy-done
  16.3 5.0 fusion.4
  21.4 70.9 %all-reduce.5.cloned.1.call-done = f32[16,1,128,128]{3,2,0,1:T(8,128)} async-done(((f32[16,1,128,128]{3,2,0,1:T(8,128)}), f32[16,1,128,128]{3,2,0,1:T(8,128)}) %all-reduce.5.cloned.1.call-update) | async-done | bytes 1048592 | tf_op jit(solution)/shard_map/psum | solution.py:52
  92.2 0.2 all-reduce.9.cloned.1.call-start
  92.5 151.5 %all-reduce.7.cloned.1.call-done = f32[16,1,128,128]{3,2,0,1:T(8,128)} async-done(((f32[16,1,128,128]{3,2,0,1:T(8,128)}), f32[16,1,128,128]{3,2,0,1:T(8,128)}) %all-reduce.7.cloned.1.call-update) | async-done | bytes 1048592 | tf_op jit(solution)/shard_map/psum | solution.py:52
  244.0 1.5 multiply_reduce_fusion.1
  245.6 2.3 fusion.15
  247.9 1.0 fusion.25
  249.0 1.3 fusion.19
  250.2 1.2 fusion.14
  251.5 1.2 fusion.35
  252.7 1.2 fusion.34
  253.8 1.2 fusion.13
  255.1 1.2 fusion.37
  256.3 1.2 fusion.36
  257.5 1.6 fusion.12
  259.1 1.2 fusion.38
  260.3 1.2 fusion.39
  261.5 1.2 fusion.11
  262.7 1.9 convolution_multiply_fusion.6
  264.6 3.8 fusion.2
  268.4 0.5 slice_bitcast_fusion.1
  268.9 1.3 copy-done.2
  270.2 5.2 fusion.5
  275.5 66.6 %all-reduce.9.cloned.1.call-done = f32[1,16,128,128]{3,2,1,0:T(8,128)} async-done(((f32[1,16,128,128]{3,2,1,0:T(8,128)}), f32[1,16,128,128]{3,2,1,0:T(8,128)}) %all-reduce.9.cloned.1.call-update) | async-done | bytes 1048592 | tf_op jit(solution)/shard_map/psum | solution.py:52
  342.1 151.6 %all-reduce.11.cloned.1.call-done = f32[1,16,128,128]{3,2,1,0:T(8,128)} async-done(((f32[1,16,128,128]{3,2,1,0:T(8,128)}), f32[1,16,128,128]{3,2,1,0:T(8,128)}) %all-reduce.11.cloned.1.call-update) | async-done | bytes 1048592 | tf_op jit(solution)/shard_map/psum | solution.py:52
  493.7 1.5 multiply_reduce_fusion
  495.3 2.3 fusion.10
  497.6 1.0 fusion.22
  498.7 1.3 fusion.16
  499.9 1.2 fusion.9
  501.2 1.2 fusion.41
  502.4 1.2 fusion.40
  503.6 1.2 fusion.8
  504.8 1.2 fusion.43
  506.0 1.2 fusion.42
  507.2 1.4 fusion.7
  508.6 1.2 fusion.44
  509.8 1.2 fusion.45
  511.0 1.2 fusion.6
  512.2 1.9 convolution_multiply_fusion
  514.1 3.8 fusion
  517.9 2.6 copy.5
  520.5 2.5 broadcast_in_dim.4
  523.1 8.3 %scatter_fusion = f32[32,64,512]{2,1,0:T(8,128)} fusion(f32[32,64,512]{2,1,0:T(8,128)} %broadcast_in_dim.4, s32[32]{0:T(128)S(1)} %compare_select_fusion, f32[32,64,512]{2,1,0:T(8,128)} %bitcast.98), kind=kCustom, calls=%fused_computation.1 | custom fusion | bytes 12583040 | tf_op jit(solution)/shard_map/scatter | solution.py:58
  (22 shorter events, 0.2 us)
Async XLA Ops:
  6.5 85.7 %all-reduce.5.cloned.1.call-start = ((), (), s32[]{:S(2)}) async-start(), calls=%async_computation | async-start | bytes 2097152 | tf_op jit(solution)/shard_map/psum | solution.py:52
  15.0 1.3 copy-start
  21.3 222.7 %all-reduce.7.cloned.1.call-start = ((), (), s32[]{:S(2)}) async-start(), calls=%async_computation.1 | async-start | bytes 2097152 | tf_op jit(solution)/shard_map/psum | solution.py:52
  92.2 249.8 %all-reduce.9.cloned.1.call-start = ((), (), s32[]{:S(2)}) async-start(), calls=%async_computation.2 | async-start | bytes 2097152 | tf_op jit(solution)/shard_map/psum | solution.py:52
  244.0 4.9 copy-start.4
  260.3 4.3 copy-start.1
  268.9 1.3 copy-start.2
  275.5 218.3 %all-reduce.11.cloned.1.call-start = ((), (), s32[]{:S(2)}) async-start(), calls=%async_computation.3 | async-start | bytes 2097152 | tf_op jit(solution)/shard_map/psum | solution.py:52
  493.7 4.9 copy-start.5
  509.8 4.3 copy-start.3
Sparse Core Ops, SparseCore 0:
  21.4 70.7 all-reduce.4
  95.7 148.3 all-reduce.6
  275.6 66.4 all-reduce.8
  345.4 148.3 all-reduce.10
